TPU v7x, 32 devices: a whole 2x2x4 slice. The times are simulated.
32 devices in a mesh: mem: 16 (over z, y, x), row: 2 (over core).
Axes of the slice: x: 2, y: 2, z: 4, core: 2. Of those that a mesh axis runs over, the one named last changes fastest.
Arguments:
- realization_stack: float32 [16, 5, 32, 256], P('mem', None, 'row'), may hold values from -6 to 6
- velocity: float32 [2, 32, 256], P(None, 'row'), may hold values from -0.25 to 0.25
- diffusion: float32 [5], replicated, may hold values from 0.04 to 0.12
- obs_cell: int32 [2048], replicated, may hold values from 0 to 40959
- obs_order: int32 [2048], replicated, may hold values from 0 to 2047, each once
- obs_value: float32 [2048], replicated, may hold values from -6 to 6
- obs_var: float32 [2048], replicated, may hold values from 0.2 to 2
- field_mask: int32 [5, 5], replicated, may hold values 0 or 1
Outputs:
- analysis: float32 [16, 5, 2, 16, 256], P(None, None, 'row', 'mem')
Inputs may be any that keep to these rules, and one draw needn't show every extreme that they name: `obs_cell`: a flat index field * 32 * 256 + row * 256 + column. `obs_order`: each of 0 to 2047 exactly once.
All inputs are finite; a program needn't handle non-finite values.
Results may differ from a plain program's by a relative error of at most 0.0003.
Values sent between devices are 32-bit elements; how exact they have to be, the bound alone decides.
No kernel may reach another device: no remote copies, remote signals or barrier semaphores. Data moves between devices by JAX's collectives and lax.ppermute only.
A program may use at most 64 MiB of HBM per device.

v0:
```python
import jax
import jax.numpy as jnp
from jax import lax
from jax.sharding import PartitionSpec as P

SUBSTEPS = 4
BATCHES = 2
LOC_HALF = 32
precise = lax.Precision.HIGHEST


def extended(shard, sides, width):
    for axis, dim in sides:
        count, length = (lax.axis_size(axis), shard.shape[dim])
        up = [(i, (i + 1) % count) for i in range(count - 1)]
        down = [(j, i) for i, j in up]
        last = lax.slice_in_dim(shard, length - width, length, axis=dim)
        initial = lax.slice_in_dim(shard, 0, width, axis=dim)
        before = lax.ppermute(last, axis, up)
        after = lax.ppermute(initial, axis, down)
        shard = jnp.concatenate([before, shard, after], axis=dim)
    return shard


def advance(padded, velocity, diffusion):
    spec_pad = ((0, 0),) * (padded.ndim - 1) + ((1, 1),)
    col_padded = jnp.pad(padded, spec_pad)
    centre = col_padded[..., 1:-1, 1:-1]
    north_cell = col_padded[..., :-2, 1:-1]
    south_cell = col_padded[..., 2:, 1:-1]
    west_cell = col_padded[..., 1:-1, :-2]
    east_cell = col_padded[..., 1:-1, 2:]
    along_col = velocity[0]
    along_row = velocity[1]
    spread = north_cell + south_cell + west_cell + east_cell - 4.0 * centre
    carried = (
        jnp.maximum(along_col, 0.0) * (centre - west_cell)
        + jnp.minimum(along_col, 0.0) * (east_cell - centre)
        + jnp.maximum(along_row, 0.0) * (centre - north_cell)
        + jnp.minimum(along_row, 0.0) * (south_cell - centre)
    )
    return centre + diffusion[:, None, None] * spread - carried


def gaspari(dist_sq):
    scaled = jnp.sqrt(dist_sq) / LOC_HALF
    clipped = jnp.maximum(scaled, 1.0)
    inner_part = (
        ((-0.25 * scaled + 0.5) * scaled + 0.625) * scaled - 5.0 / 3.0
    ) * scaled * scaled + 1.0
    outer_part = (
        ((((scaled / 12.0 - 0.5) * scaled + 0.625) * scaled + 5.0 / 3.0) * scaled - 5.0) * scaled
        + 4.0
        - 2.0 / (3.0 * clipped)
    )
    return jnp.where(scaled <= 1.0, inner_part, jnp.where(scaled <= 2.0, outer_part, 0.0))


def decode(flat_cells, total_rows, n_cols):
    field_ids = flat_cells // (total_rows * n_cols)
    row_ids = flat_cells // n_cols % total_rows
    col_ids = flat_cells % n_cols
    return (field_ids, row_ids, col_ids)


def innovations(priors, obs_values, obs_noise):
    members = priors.shape[0]
    average = jnp.mean(priors, axis=0)
    anomaly = priors - average
    spread = jnp.sum(anomaly * anomaly, axis=0) / (members - 1)
    variance_sum = spread + obs_noise
    root_sum = jnp.sqrt(variance_sum)
    shrink = 1.0 / (root_sum * (jnp.sqrt(obs_noise) + root_sum))
    adjust = (obs_values - average) / variance_sum - shrink * anomaly
    return (anomaly, adjust)


def regress(
    ensemble_now, base_row, obs_field, obs_row, obs_col, anomaly, adjust, field_mask, n_cols
):
    members, n_cells = ensemble_now.shape
    n_fields = field_mask.shape[0]
    per_field = n_cells // n_fields
    local_ids = lax.iota(jnp.int32, per_field)
    cell_row = (base_row + local_ids // n_cols).astype(jnp.float32)
    cell_col = (local_ids % n_cols).astype(jnp.float32)
    centred = ensemble_now - jnp.mean(ensemble_now, axis=0)
    mask_float = field_mask.astype(jnp.float32)
    total_obs = obs_field.shape[0]
    obs_block = min(256, total_obs)
    increment = jnp.zeros_like(ensemble_now)
    for offset in range(0, total_obs, obs_block):
        row_gap = cell_row[:, None] - obs_row[None, offset : offset + obs_block].astype(jnp.float32)
        col_gap = cell_col[:, None] - obs_col[None, offset : offset + obs_block].astype(jnp.float32)
        closeness = gaspari(row_gap * row_gap + col_gap * col_gap)
        field_hot = (
            obs_field[None, offset : offset + obs_block] == lax.iota(jnp.int32, n_fields)[:, None]
        ).astype(jnp.float32)
        allowed = jnp.dot(mask_float, field_hot, precision=precise)
        covariance = lax.dot_general(
            centred,
            anomaly[:, offset : offset + obs_block],
            (((0,), (0,)), ((), ())),
            precision=precise,
        )
        weights = (
            covariance.reshape(n_fields, per_field, obs_block)
            * (closeness[None] * allowed[:, None, :])
            / (members - 1)
        )
        increment = increment + lax.dot_general(
            adjust[:, offset : offset + obs_block],
            weights.reshape(n_cells, obs_block),
            (((1,), (1,)), ((), ())),
            precision=precise,
        )
    return ensemble_now + increment


def per_device(
    realization_stack, velocity, diffusion, obs_cell, obs_order, obs_value, obs_var, field_mask
):
    local_members = realization_stack.shape[0]
    n_fields = realization_stack.shape[1]
    rows_here = realization_stack.shape[2]
    n_cols = realization_stack.shape[3]
    n_mem = lax.axis_size("mem")
    n_slab = lax.axis_size("row")
    total_members = local_members * n_mem
    total_rows = rows_here * n_slab
    slab_index = lax.axis_index("row")
    member_index = lax.axis_index("mem")
    row_sub = rows_here // n_mem
    current = realization_stack
    for substep in range(SUBSTEPS):
        padded = extended(current, (("row", 2),), 1)
        current = advance(padded, velocity, diffusion)
    field_all, row_all, col_all = decode(obs_cell, total_rows, n_cols)
    batch_size = obs_cell.shape[0] // BATCHES
    layout = lax.all_to_all(current, "mem", split_axis=2, concat_axis=0, tiled=True)
    ensemble_now = layout.reshape(total_members, -1)
    base_row = slab_index * rows_here + member_index * row_sub
    for batch_num in range(BATCHES):
        picked = obs_order[batch_num * batch_size : (batch_num + 1) * batch_size]
        obs_field = field_all[picked]
        obs_row = row_all[picked]
        obs_col = col_all[picked]
        owned = ((obs_row >= base_row) & (obs_row < base_row + row_sub)).astype(jnp.float32)
        local_ids = (
            obs_field * row_sub * n_cols
            + jnp.clip(obs_row - base_row, 0, row_sub - 1) * n_cols
            + obs_col
        )
        partial_priors = jnp.take(ensemble_now, local_ids, axis=1) * owned[None, :]
        priors = lax.psum(partial_priors, ("mem", "row"))
        anomaly, adjust = innovations(priors, obs_value[picked], obs_var[picked])
        ensemble_now = regress(
            ensemble_now, base_row, obs_field, obs_row, obs_col, anomaly, adjust, field_mask, n_cols
        )
    return ensemble_now.reshape(total_members, n_fields, 1, row_sub, n_cols)


def solution(mesh):
    in_specs = (P("mem", None, "row", None), P(None, "row", None), P(), P(), P(), P(), P(), P())
    out_specs = P(None, None, "row", "mem", None)
    return jax.shard_map(
        per_device, mesh=mesh, in_specs=in_specs, out_specs=out_specs, check_vma=False
    )
```

profile of v0, /device:TPU:0, one launch (start us, length us, event | category | flops | bytes accessed | tf_op | source)
XLA Modules:
  0.0 403.0 jit_solution(6026265140585205028)
XLA Ops:
  7.5 1.3 collective-permute-start.1
  8.8 3.0 collective-permute-start
  13.3 6.1 %gather_fusion.8 = s32[1024]{0:T(1024)S(1)} fusion(s32[2048]{0:T(1024)S(1)} %get-tuple-element.33, s32[1024]{0:T(1024)S(1)} %get-tuple-element.28), kind=kCustom, calls=%fused_computation.10 | custom fusion | bytes 12288 | tf_op jit(solution)/shard_map/gather | solution.py:147
  19.4 6.2 %gather_fusion.7 = s32[1024]{0:T(1024)S(1)} fusion(s32[2048]{0:T(1024)S(1)} %get-tuple-element.32, s32[1024]{0:T(1024)S(1)} %get-tuple-element.28), kind=kCustom, calls=%fused_computation.9 | custom fusion | bytes 12288 | tf_op jit(solution)/shard_map/gather | solution.py:146
  25.6 6.2 %gather_fusion.3 = s32[1024]{0:T(1024)S(1)} fusion(s32[2048]{0:T(1024)S(1)} %get-tuple-element.33, s32[1024]{0:T(1024)S(1)} %get-tuple-element.29), kind=kCustom, calls=%fused_computation.5 | custom fusion | bytes 12288 | tf_op jit(solution)/shard_map/gather | solution.py:147
  31.8 6.2 %gather_fusion.2 = s32[1024]{0:T(1024)S(1)} fusion(s32[2048]{0:T(1024)S(1)} %get-tuple-element.32, s32[1024]{0:T(1024)S(1)} %get-tuple-element.29), kind=kCustom, calls=%fused_computation.4 | custom fusion | bytes 12288 | tf_op jit(solution)/shard_map/gather | solution.py:146
  37.9 6.2 %gather_fusion.1 = s32[1024]{0:T(1024)S(1)} fusion(s32[2048]{0:T(1024)S(1)} %get-tuple-element.34, s32[1024]{0:T(1024)S(1)} %get-tuple-element.29), kind=kCustom, calls=%fused_computation.3 | custom fusion | bytes 12288 | tf_op jit(solution)/shard_map/gather | solution.py:145
  44.1 6.2 %gather_fusion.6 = s32[1024]{0:T(1024)S(1)} fusion(s32[2048]{0:T(1024)S(1)} %get-tuple-element.34, s32[1024]{0:T(1024)S(1)} %get-tuple-element.28), kind=kCustom, calls=%fused_computation.8 | custom fusion | bytes 12288 | tf_op jit(solution)/shard_map/gather | solution.py:145
  51.1 3.7 fusion.25
  55.0 1.7 broadcast_multiply_fusion
  57.2 1.3 collective-permute-start.3
  58.5 3.0 collective-permute-start.2
  62.6 1.3 collective-permute-start.5
  63.9 3.0 collective-permute-start.4
  68.0 1.3 collective-permute-start.7
  69.3 3.0 collective-permute-start.6
  72.4 6.2 %gather_fusion = f32[1024]{0:T(1024)S(1)} fusion(f32[2048]{0:T(1024)S(1)} %copy-done, s32[1024]{0:T(1024)S(1)} %get-tuple-element.29), kind=kCustom, calls=%fused_computation.2 | custom fusion | bytes 12288 | tf_op jit(solution)/shard_map/gather | solution.py:156
  78.6 6.2 %gather_fusion.5 = f32[1024]{0:T(1024)S(1)} fusion(f32[2048]{0:T(1024)S(1)} %copy-done, s32[1024]{0:T(1024)S(1)} %get-tuple-element.28), kind=kCustom, calls=%fused_computation.7 | custom fusion | bytes 12288 | tf_op jit(solution)/shard_map/gather | solution.py:156
  84.7 6.2 %gather_fusion.4 = f32[1024]{0:T(1024)S(1)} fusion(f32[2048]{0:T(1024)S(1)} %copy-done.1, s32[1024]{0:T(1024)S(1)} %get-tuple-element.29), kind=kCustom, calls=%fused_computation.6 | custom fusion | bytes 12288 | tf_op jit(solution)/shard_map/gather | solution.py:156
  90.9 6.2 %gather_fusion.9 = f32[1024]{0:T(1024)S(1)} fusion(f32[2048]{0:T(1024)S(1)} %copy-done.1, s32[1024]{0:T(1024)S(1)} %get-tuple-element.28), kind=kCustom, calls=%fused_computation.11 | custom fusion | bytes 12288 | tf_op jit(solution)/shard_map/gather | solution.py:156
  98.0 8.3 %all-to-all-start = ((f32[1,5,16,256]{3,1,0,2:T(8,128)}), f32[1,5,16,256]{3,1,0,2:T(8,128)S(1)}, u32[]{:S(2)}, u32[]{:S(2)}) async-start(f32[1,5,16,256]{3,1,0,2:T(8,128)} %fusion.48), calls=%async_computation | async-start | bytes 262144 | tf_op jit(solution)/shard_map/all_to_all | solution.py:140
  106.4 7.7 %all-to-all-done = f32[1,5,16,256]{3,1,0,2:T(8,128)S(1)} async-done(((f32[1,5,16,256]{3,1,0,2:T(8,128)}), f32[1,5,16,256]{3,1,0,2:T(8,128)S(1)}, u32[]{:S(2)}, u32[]{:S(2)}) %all-to-all-start) | async-done | bytes 81952 | tf_op jit(solution)/shard_map/all_to_all | solution.py:140
  114.4 4.0 gather_fusion.10
  120.6 114.6 %all-reduce.7.cloned.1.call-done = f32[16,1024]{1,0:T(8,128)} async-done(((f32[16,1024]{1,0:T(8,128)}), f32[16,1024]{1,0:T(8,128)}) %all-reduce.7.cloned.1.call-update) | async-done | bytes 65552 | tf_op jit(solution)/shard_map/psum | solution.py:155
  247.1 4.2 %gather_fusion.11 = f32[1024,16]{1,0:T(8,128)} fusion(f32[16,1280]{0,1:T(8,128)S(1)} %copy.44, s32[1024]{0:T(1024)S(1)} %broadcast_clamp_fusion), kind=kCustom, calls=%fused_computation.1.clone | custom fusion | bytes 135168 | tf_op jit(solution)/shard_map/jit(_take)/gather | solution.py:154
  251.3 2.2 bitcast_multiply_fusion
  253.5 128.8 %all-reduce.9.cloned.1.call-done = f32[16,1024]{0,1:T(8,128)} async-done(((f32[16,1024]{0,1:T(8,128)}), f32[16,1024]{0,1:T(8,128)}) %all-reduce.9.cloned.1.call-update) | async-done | bytes 65552 | tf_op jit(solution)/shard_map/psum | solution.py:155
  383.5 1.4 multiply_reduce_fusion
  384.9 1.3 fusion
  391.7 1.3 convolution_add_fusion.2
  392.9 1.3 convolution_add_fusion.1
  394.2 1.3 fusion.4
  (102 shorter events, 28.5 us)
Async XLA Ops:
  6.5 65.8 %copy-start = (f32[2048]{0:T(1024)S(1)}, f32[2048]{0:T(1024)}, u32[]{:S(2)}) copy-start(f32[2048]{0:T(1024)} %param.15) | copy-start | bytes 24580
  7.5 49.4 %collective-permute-start.1 = (f32[1,5,1,256]{3,1,0,2:T(8,128)S(1)}, f32[1,5,1,256]{3,1,0,2:T(8,128)S(1)}, u32[]{:S(2)}, u32[]{:S(2)}) collective-permute-start(f32[1,5,1,256]{3,1,0,2:T(8,128)S(1)} %get-tuple-element.21), channel_id=1, source_target_pairs={{1,0},{3,2},{5,4},{7,6},{9,8},{11,10},{13,12},{15,14},{17,16},{19,... | collective-permute-start | bytes 15368 | tf_op jit(solution)/shard_map/ppermute | solution.py:20
  8.8 48.1 %collective-permute-start = (f32[1,5,1,256]{3,1,0,2:T(8,128)S(1)}, f32[1,5,1,256]{3,1,0,2:T(8,128)S(1)}, u32[]{:S(2)}, u32[]{:S(2)}) collective-permute-start(f32[1,5,1,256]{3,1,0,2:T(8,128)S(1)} %get-tuple-element.20), channel_id=1, source_target_pairs={{0,1},{2,3},{4,5},{6,7},{8,9},{10,11},{12,13},{14,15},{16,17},{18,... | collective-permute-start | bytes 15368 | tf_op jit(solution)/shard_map/ppermute | solution.py:19
  44.1 6.2 %copy-start.9 = (f32[2,16,256]{2,1,0:T(8,128)S(1)}, f32[2,16,256]{2,1,0:T(8,128)}, u32[]{:S(2)}) copy-start(f32[2,16,256]{2,1,0:T(8,128)} %param.11) | copy-start | bytes 98308
  44.1 6.3 %copy-start.8 = (s32[5,5]{1,0:T(8,128)S(1)}, s32[5,5]{1,0:T(8,128)}, u32[]{:S(2)}) copy-start(s32[5,5]{1,0:T(8,128)} %param.17) | copy-start | bytes 304
  55.0 2.0 copy-start.10
  57.2 4.5 %collective-permute-start.3 = (f32[1,5,1,256]{3,1,0,2:T(8,128)S(1)}, f32[1,5,1,256]{3,1,0,2:T(8,128)S(1)}, u32[]{:S(2)}, u32[]{:S(2)}) collective-permute-start(f32[1,5,1,256]{3,1,0,2:T(8,128)S(1)} %get-tuple-element.19), channel_id=1, source_target_pairs={{1,0},{3,2},{5,4},{7,6},{9,8},{11,10},{13,12},{15,14},{17,16},{19,... | collective-permute-start | bytes 15368 | tf_op jit(solution)/shard_map/ppermute | solution.py:20
  58.5 3.8 collective-permute-start.2
  62.6 4.5 %collective-permute-start.5 = (f32[1,5,1,256]{3,1,0,2:T(8,128)S(1)}, f32[1,5,1,256]{3,1,0,2:T(8,128)S(1)}, u32[]{:S(2)}, u32[]{:S(2)}) collective-permute-start(f32[1,5,1,256]{3,1,0,2:T(8,128)S(1)} %get-tuple-element.17), channel_id=1, source_target_pairs={{1,0},{3,2},{5,4},{7,6},{9,8},{11,10},{13,12},{15,14},{17,16},{19,... | collective-permute-start | bytes 15368 | tf_op jit(solution)/shard_map/ppermute | solution.py:20
  63.9 3.8 collective-permute-start.4
  68.0 29.0 %collective-permute-start.7 = (f32[1,5,1,256]{3,1,0,2:T(8,128)S(1)}, f32[1,5,1,256]{3,1,0,2:T(8,128)S(1)}, u32[]{:S(2)}, u32[]{:S(2)}) collective-permute-start(f32[1,5,1,256]{3,1,0,2:T(8,128)S(1)} %get-tuple-element.15), channel_id=1, source_target_pairs={{1,0},{3,2},{5,4},{7,6},{9,8},{11,10},{13,12},{15,14},{17,16},{19,... | collective-permute-start | bytes 15368 | tf_op jit(solution)/shard_map/ppermute | solution.py:20
  69.3 27.7 %collective-permute-start.6 = (f32[1,5,1,256]{3,1,0,2:T(8,128)S(1)}, f32[1,5,1,256]{3,1,0,2:T(8,128)S(1)}, u32[]{:S(2)}, u32[]{:S(2)}) collective-permute-start(f32[1,5,1,256]{3,1,0,2:T(8,128)S(1)} %get-tuple-element.14), channel_id=1, source_target_pairs={{0,1},{2,3},{4,5},{6,7},{8,9},{10,11},{12,13},{14,15},{16,17},{18,... | collective-permute-start | bytes 15368 | tf_op jit(solution)/shard_map/ppermute | solution.py:19
  78.6 6.2 %copy-start.1 = (f32[2048]{0:T(1024)S(1)}, f32[2048]{0:T(1024)}, u32[]{:S(2)}) copy-start(f32[2048]{0:T(1024)} %param.16) | copy-start | bytes 24580
  98.0 16.1 %all-to-all-start = ((f32[1,5,16,256]{3,1,0,2:T(8,128)}), f32[1,5,16,256]{3,1,0,2:T(8,128)S(1)}, u32[]{:S(2)}, u32[]{:S(2)}) async-start(f32[1,5,16,256]{3,1,0,2:T(8,128)} %fusion.48), calls=%async_computation | async-start | bytes 262144 | tf_op jit(solution)/shard_map/all_to_all | solution.py:140
  106.3 128.8 %all-reduce.7.cloned.1.call-start = ((), (), s32[]{:S(2)}) async-start(), calls=%async_computation.1 | async-start | bytes 131072 | tf_op jit(solution)/shard_map/psum | solution.py:155
  118.4 118.5 %copy-start.7 = (f32[256,256]{1,0:T(8,128)S(1)}, f32[256,256]{1,0:T(8,128)}, u32[]{:S(2)}) copy-start(f32[256,256]{1,0:T(8,128)} %get-tuple-element.68) | copy-start | bytes 786436
  120.3 261.9 %all-reduce.9.cloned.1.call-start = ((), (), s32[]{:S(2)}) async-start(), calls=%async_computation.2 | async-start | bytes 1048576 | tf_op jit(solution)/shard_map/psum | solution.py:155
  236.9 2.5 copy-start.6
  239.4 2.5 copy-start.5
  241.9 2.5 copy-start.4
  386.2 1.3 copy-start.3
  387.5 1.3 copy-start.2
Sparse Core Ops, SparseCore 0:
  120.5 114.6 all-reduce.6
  253.6 128.6 all-reduce.8
where the time goes:
time: 404 us; the launch traced here: 403 us
  waiting for transfers between devices  253 us (63%)
  local copies, waits for them, and re-layouts  73.4 us (18%)
  starting transfers between devices  25.9 us (6%)
  matrix products  20.7 us (5%)
  other arithmetic  16.5 us (4%)
  between operations  14.1 us (3%)
    psum x2, waiting for transfers between devices, per_device(): priors = lax.psum(partial_priors, ('mem', 'row'))  243 us
    gather x4, local copies, waits for them, and re-layouts, per_device(): anomaly, adjust = innovations(priors, obs_value[picked], obs_var[picked])  24.6 us
    gather x2, local copies, waits for them, and re-layouts, per_device(): obs_field = field_all[picked]  12.3 us
    gather x2, local copies, waits for them, and re-layouts, per_device(): obs_row = row_all[picked]  12.3 us
    gather x2, local copies, waits for them, and re-layouts, per_device(): obs_col = col_all[picked]  12.3 us
    ppermute x4, starting transfers between devices, extended(): before = lax.ppermute(last, axis, up)  12.1 us
    dot_general x8, matrix products, regress(): lax.dot_general(centred, anomaly[:, offset:offset + obs_block], (((0,), (...  9.99 us
    dot_general x8, matrix products, regress(): lax.dot_general(adjust[:, offset:offset + obs_block], weights.reshape(n_c...  9.76 us
  transfers between devices with their start and end apart: 11, of which 5 were waited for; matrix products, arithmetic and copies ran while one was open for 17% of the time, Pallas kernels for 0%

commit v1 on v0

--- a/solution.py
+++ b/solution.py
@@ -152,7 +152,8 @@
             + obs_col
         )
         partial_priors = jnp.take(ensemble_now, local_ids, axis=1) * owned[None, :]
-        priors = lax.psum(partial_priors, ("mem", "row"))
+        f_now = jax.lax.all_gather(partial_priors, ("mem", "row"))
+        priors = jnp.sum(f_now, axis=0)
         anomaly, adjust = innovations(priors, obs_value[picked], obs_var[picked])
         ensemble_now = regress(
             ensemble_now, base_row, obs_field, obs_row, obs_col, anomaly, adjust, field_mask, n_cols

time: 404 us -> 237 us (0.59)
  waiting for transfers between devices: 253 us -> 86 us
    psum x2 -> x0, waiting for transfers between devices: 243 us -> none  [per_device(): priors = lax.psum(partial_priors, ('mem', 'row'))]
    all_gather x0 -> x2, waiting for transfers between devices: none -> 76.5 us  [per_device(): f_now = jax.lax.all_gather(partial_priors, ('mem', 'row'))]
    reduce_sum x0 -> x2, other arithmetic: none -> 4.33 us  [per_device(): priors = jnp.sum(f_now, axis=0)]
    gather x3 -> x4, local copies, waits for them, and re-layouts: 9.46 us -> 5.96 us  [per_device(): partial_priors = jnp.take(ensemble_now, local_ids, axis=1) * owned[None, :]]
  transfers between devices with their start and end apart: 11 -> 11, of which waited for: 5 -> 6; matrix products, arithmetic and copies ran while one was open for 17% -> 30% of each run, Pallas kernels for 0% -> 0%
where the time goes in v1:
time: 237 us; the launch traced here: 236 us
  waiting for transfers between devices  86 us (36%)
  local copies, waits for them, and re-layouts  70.5 us (30%)
  starting transfers between devices  25.9 us (11%)
  matrix products  22.7 us (10%)
  other arithmetic  16.9 us (7%)
  between operations  14.1 us (6%)
    all_gather x2, waiting for transfers between devices, per_device(): f_now = jax.lax.all_gather(partial_priors, ('mem', 'row'))  76.5 us
    gather x4, local copies, waits for them, and re-layouts, per_device(): anomaly, adjust = innovations(priors, obs_value[picked], obs_var[picked])  24.8 us
    gather x2, local copies, waits for them, and re-layouts, per_device(): obs_col = col_all[picked]  12.3 us
    gather x2, local copies, waits for them, and re-layouts, per_device(): obs_row = row_all[picked]  12.3 us
    gather x2, local copies, waits for them, and re-layouts, per_device(): obs_field = field_all[picked]  12.3 us
    dot_general x8, matrix products, regress(): lax.dot_general(centred, anomaly[:, offset:offset + obs_block], (((0,), (...  12.2 us
    ppermute x4, starting transfers between devices, extended(): before = lax.ppermute(last, axis, up)  12.1 us
    dot_general x8, matrix products, regress(): lax.dot_general(adjust[:, offset:offset + obs_block], weights.reshape(n_c...  9.47 us
  transfers between devices with their start and end apart: 11, of which 6 were waited for; matrix products, arithmetic and copies ran while one was open for 30% of the time, Pallas kernels for 0%

profile of v1, /device:TPU:0, one launch (start us, length us, event | category | flops | bytes accessed | tf_op | source)
XLA Modules:
  0.0 236.0 jit_solution(7131072668330672747)
XLA Ops:
  7.5 1.3 collective-permute-start.1
  8.8 3.0 %collective-permute-start = (f32[1,5,1,256]{3,1,0,2:T(8,128)S(1)}, f32[1,5,1,256]{3,1,0,2:T(8,128)S(1)}, u32[]{:S(2)}, u32[]{:S(2)}) collective-permute-start(f32[1,5,1,256]{3,1,0,2:T(8,128)S(1)} %get-tuple-element.20), channel_id=1, source_target_pairs={{0,1},{2,3},{4,5},{6,7},{8,9},{10,11},{12,13},{14,15},{16,17},{18,... | collective-permute-start | bytes 15368 | tf_op jit(solution)/shard_map/ppermute | solution.py:19
  13.6 1.3 collective-permute-start.3
  14.9 3.0 %collective-permute-start.2 = (f32[1,5,1,256]{3,1,0,2:T(8,128)S(1)}, f32[1,5,1,256]{3,1,0,2:T(8,128)S(1)}, u32[]{:S(2)}, u32[]{:S(2)}) collective-permute-start(f32[1,5,1,256]{3,1,0,2:T(8,128)S(1)} %get-tuple-element.18), channel_id=1, source_target_pairs={{0,1},{2,3},{4,5},{6,7},{8,9},{10,11},{12,13},{14,15},{16,17},{18,... | collective-permute-start | bytes 15368 | tf_op jit(solution)/shard_map/ppermute | solution.py:19
  19.1 1.3 collective-permute-start.5
  20.4 3.0 %collective-permute-start.4 = (f32[1,5,1,256]{3,1,0,2:T(8,128)S(1)}, f32[1,5,1,256]{3,1,0,2:T(8,128)S(1)}, u32[]{:S(2)}, u32[]{:S(2)}) collective-permute-start(f32[1,5,1,256]{3,1,0,2:T(8,128)S(1)} %get-tuple-element.16), channel_id=1, source_target_pairs={{0,1},{2,3},{4,5},{6,7},{8,9},{10,11},{12,13},{14,15},{16,17},{18,... | collective-permute-start | bytes 15368 | tf_op jit(solution)/shard_map/ppermute | solution.py:19
  23.4 6.2 %gather_fusion.8 = s32[1024]{0:T(1024)S(1)} fusion(s32[2048]{0:T(1024)S(1)} %get-tuple-element.33, s32[1024]{0:T(1024)S(1)} %get-tuple-element.28), kind=kCustom, calls=%fused_computation.10 | custom fusion | bytes 12288 | tf_op jit(solution)/shard_map/gather | solution.py:147
  29.6 6.2 %gather_fusion.7 = s32[1024]{0:T(1024)S(1)} fusion(s32[2048]{0:T(1024)S(1)} %get-tuple-element.32, s32[1024]{0:T(1024)S(1)} %get-tuple-element.28), kind=kCustom, calls=%fused_computation.9 | custom fusion | bytes 12288 | tf_op jit(solution)/shard_map/gather | solution.py:146
  35.7 6.2 %gather_fusion.3 = s32[1024]{0:T(1024)S(1)} fusion(s32[2048]{0:T(1024)S(1)} %get-tuple-element.33, s32[1024]{0:T(1024)S(1)} %get-tuple-element.29), kind=kCustom, calls=%fused_computation.5 | custom fusion | bytes 12288 | tf_op jit(solution)/shard_map/gather | solution.py:147
  41.9 6.2 %gather_fusion.2 = s32[1024]{0:T(1024)S(1)} fusion(s32[2048]{0:T(1024)S(1)} %get-tuple-element.32, s32[1024]{0:T(1024)S(1)} %get-tuple-element.29), kind=kCustom, calls=%fused_computation.4 | custom fusion | bytes 12288 | tf_op jit(solution)/shard_map/gather | solution.py:146
  48.1 6.2 %gather_fusion.1 = s32[1024]{0:T(1024)S(1)} fusion(s32[2048]{0:T(1024)S(1)} %get-tuple-element.34, s32[1024]{0:T(1024)S(1)} %get-tuple-element.29), kind=kCustom, calls=%fused_computation.3 | custom fusion | bytes 12288 | tf_op jit(solution)/shard_map/gather | solution.py:145
  54.2 6.2 %gather_fusion.6 = s32[1024]{0:T(1024)S(1)} fusion(s32[2048]{0:T(1024)S(1)} %get-tuple-element.34, s32[1024]{0:T(1024)S(1)} %get-tuple-element.28), kind=kCustom, calls=%fused_computation.8 | custom fusion | bytes 12288 | tf_op jit(solution)/shard_map/gather | solution.py:145
  60.7 1.3 collective-permute-start.7
  62.0 3.0 %collective-permute-start.6 = (f32[1,5,1,256]{3,1,0,2:T(8,128)S(1)}, f32[1,5,1,256]{3,1,0,2:T(8,128)S(1)}, u32[]{:S(2)}, u32[]{:S(2)}) collective-permute-start(f32[1,5,1,256]{3,1,0,2:T(8,128)S(1)} %get-tuple-element.14), channel_id=1, source_target_pairs={{0,1},{2,3},{4,5},{6,7},{8,9},{10,11},{12,13},{14,15},{16,17},{18,... | collective-permute-start | bytes 15368 | tf_op jit(solution)/shard_map/ppermute | solution.py:19
  66.8 8.3 %all-to-all-start = ((f32[1,5,16,256]{3,1,0,2:T(8,128)}), f32[1,5,16,256]{3,1,0,2:T(8,128)S(1)}, u32[]{:S(2)}, u32[]{:S(2)}) async-start(f32[1,5,16,256]{3,1,0,2:T(8,128)} %fusion.39), calls=%async_computation | async-start | bytes 262144 | tf_op jit(solution)/shard_map/all_to_all | solution.py:140
  75.1 7.9 %all-to-all-done = f32[1,5,16,256]{3,1,0,2:T(8,128)S(1)} async-done(((f32[1,5,16,256]{3,1,0,2:T(8,128)}), f32[1,5,16,256]{3,1,0,2:T(8,128)S(1)}, u32[]{:S(2)}, u32[]{:S(2)}) %all-to-all-start) | async-done | bytes 81952 | tf_op jit(solution)/shard_map/all_to_all | solution.py:140
  83.3 2.8 %gather_fusion.10 = f32[1024,16]{1,0:T(8,128)S(1)} fusion(f32[16,1280]{0,1:T(8,128)S(1)} %copy.78, s32[1024]{0:T(1024)S(1)} %broadcast_clamp_fusion.1), kind=kCustom, calls=%fused_computation.clone | custom fusion | bytes 135168 | tf_op jit(solution)/shard_map/jit(_take)/gather | solution.py:154
  87.2 6.2 %gather_fusion = f32[1024]{0:T(1024)S(1)} fusion(f32[2048]{0:T(1024)S(1)} %copy-done, s32[1024]{0:T(1024)S(1)} %get-tuple-element.29), kind=kCustom, calls=%fused_computation.2 | custom fusion | bytes 12288 | tf_op jit(solution)/shard_map/gather | solution.py:157
  93.4 6.2 %gather_fusion.4 = f32[1024]{0:T(1024)S(1)} fusion(f32[2048]{0:T(1024)S(1)} %copy-done.1, s32[1024]{0:T(1024)S(1)} %get-tuple-element.29), kind=kCustom, calls=%fused_computation.6 | custom fusion | bytes 12288 | tf_op jit(solution)/shard_map/gather | solution.py:157
  100.2 3.7 %fusion.25 = (f32[256,256]{1,0:T(8,128)S(1)}, f32[256,256]{1,0:T(8,128)}, f32[256,256]{1,0:T(8,128)}, f32[256,256]{1,0:T(8,128)}, f32[256,256]{1,0:T(8,128)S(1)}...) fusion(f32[256]{0:T(256)S(1)} %get-tuple-element.39, f32[256]{0:T(256)S(1)} %get-tuple-element.35, ...), kind=kLoop, calls=%fused_computation.73 | loop fusion | flops 17301504 | bytes 2115584 | tf_op jit(solution)/shard_map/jit(_where)/select_n | solution.py:56
  103.9 37.2 %all-gather.5.cloned.1.call-done = f32[512,1024]{1,0:T(8,128)} async-done(((f32[16,1024]{1,0:T(8,128)}), f32[512,1024]{1,0:T(8,128)}) %all-gather.5.cloned.1.call-update) | async-done | bytes 2097168 | tf_op jit(solution)/shard_map/all_gather | solution.py:155
  141.1 1.9 reduce_sum.73
  143.5 2.2 fusion.9
  147.0 1.2 fusion.8
  154.6 2.8 %gather_fusion.11 = f32[1024,16]{1,0:T(8,128)S(1)} fusion(f32[16,1280]{0,1:T(8,128)S(1)} %copy.84, s32[1024]{0:T(1024)S(1)} %broadcast_clamp_fusion), kind=kCustom, calls=%fused_computation.1.clone | custom fusion | bytes 135168 | tf_op jit(solution)/shard_map/jit(_take)/gather | solution.py:154
  158.2 6.4 %gather_fusion.5 = f32[1024]{0:T(1024)S(1)} fusion(f32[2048]{0:T(1024)S(1)} %copy-done, s32[1024]{0:T(1024)S(1)} %get-tuple-element.28), kind=kCustom, calls=%fused_computation.7 | custom fusion | bytes 12288 | tf_op jit(solution)/shard_map/gather | solution.py:157
  164.6 6.2 %gather_fusion.9 = f32[1024]{0:T(1024)S(1)} fusion(f32[2048]{0:T(1024)S(1)} %copy-done.1, s32[1024]{0:T(1024)S(1)} %get-tuple-element.28), kind=kCustom, calls=%fused_computation.11 | custom fusion | bytes 12288 | tf_op jit(solution)/shard_map/gather | solution.py:157
  171.3 1.3 broadcast_multiply_fusion.2
  172.6 1.7 broadcast_multiply_fusion
  174.4 39.3 %all-gather.7.cloned.1.call-done = f32[512,1024]{1,0:T(8,128)} async-done(((f32[16,1024]{1,0:T(8,128)}), f32[512,1024]{1,0:T(8,128)}) %all-gather.7.cloned.1.call-update) | async-done | bytes 2097168 | tf_op jit(solution)/shard_map/all_gather | solution.py:155
  213.7 2.5 %reduce_sum.77 = f32[16,1024]{1,0:T(8,128)} reduce(f32[32,16,1024]{2,1,0:T(8,128)} %bitcast.78, f32[]{:T(128)} %constant.177.clone.1), dimensions={0}, to_apply=%region_5.7 | reduce | flops 507904 | bytes 2162692 | tf_op jit(solution)/shard_map/reduce_sum | solution.py:156
  217.2 2.6 %fusion = f32[1280,256]{1,0:T(8,128)S(1)} fusion(f32[1280,256]{1,0:T(8,128)} %bitcast.80, f32[16,1280]{1,0:T(8,128)S(1)} %get-tuple-element.70, f32[1280]{0:T(1024)S(1)} %broadcast_multiply_fusion.4, f32[16,1024]{1,0:T(8,128)S(1)} %get-tuple-element.7), kind=kOutput, calls=%fused_computation.16 | convolution fusion | flops 63590400 | bytes 2727936 | tf_op jit(solution)/shard_map/dot_general | solution.py:100
  (109 shorter events, 27.4 us)
Async XLA Ops:
  6.5 80.7 %copy-start = (f32[2048]{0:T(1024)S(1)}, f32[2048]{0:T(1024)}, u32[]{:S(2)}) copy-start(f32[2048]{0:T(1024)} %param.15) | copy-start | bytes 24580
  6.5 12.4 %copy-start.12 = (f32[5]{0:T(128)S(1)}, f32[5]{0:T(128)}, u32[]{:S(2)}) copy-start(f32[5]{0:T(128)} %param.12) | copy-start | bytes 64
  6.5 11.4 %copy-start.11 = (s32[2048]{0:T(1024)S(1)}, s32[2048]{0:T(1024)}, u32[]{:S(2)}) copy-start(s32[2048]{0:T(1024)} %param.13) | copy-start | bytes 24580
  6.5 16.8 %copy-start.10 = (s32[2048]{0:T(1024)S(1)}, s32[2048]{0:T(1024)}, u32[]{:S(2)}) copy-start(s32[2048]{0:T(1024)} %param.14) | copy-start | bytes 24580
  7.5 5.1 %collective-permute-start.1 = (f32[1,5,1,256]{3,1,0,2:T(8,128)S(1)}, f32[1,5,1,256]{3,1,0,2:T(8,128)S(1)}, u32[]{:S(2)}, u32[]{:S(2)}) collective-permute-start(f32[1,5,1,256]{3,1,0,2:T(8,128)S(1)} %get-tuple-element.21), channel_id=1, source_target_pairs={{1,0},{3,2},{5,4},{7,6},{9,8},{11,10},{13,12},{15,14},{17,16},{19,... | collective-permute-start | bytes 15368 | tf_op jit(solution)/shard_map/ppermute | solution.py:20
  8.8 3.8 %collective-permute-start = (f32[1,5,1,256]{3,1,0,2:T(8,128)S(1)}, f32[1,5,1,256]{3,1,0,2:T(8,128)S(1)}, u32[]{:S(2)}, u32[]{:S(2)}) collective-permute-start(f32[1,5,1,256]{3,1,0,2:T(8,128)S(1)} %get-tuple-element.20), channel_id=1, source_target_pairs={{0,1},{2,3},{4,5},{6,7},{8,9},{10,11},{12,13},{14,15},{16,17},{18,... | collective-permute-start | bytes 15368 | tf_op jit(solution)/shard_map/ppermute | solution.py:19
  13.6 4.4 %collective-permute-start.3 = (f32[1,5,1,256]{3,1,0,2:T(8,128)S(1)}, f32[1,5,1,256]{3,1,0,2:T(8,128)S(1)}, u32[]{:S(2)}, u32[]{:S(2)}) collective-permute-start(f32[1,5,1,256]{3,1,0,2:T(8,128)S(1)} %get-tuple-element.19), channel_id=1, source_target_pairs={{1,0},{3,2},{5,4},{7,6},{9,8},{11,10},{13,12},{15,14},{17,16},{19,... | collective-permute-start | bytes 15368 | tf_op jit(solution)/shard_map/ppermute | solution.py:20
  14.9 3.8 %collective-permute-start.2 = (f32[1,5,1,256]{3,1,0,2:T(8,128)S(1)}, f32[1,5,1,256]{3,1,0,2:T(8,128)S(1)}, u32[]{:S(2)}, u32[]{:S(2)}) collective-permute-start(f32[1,5,1,256]{3,1,0,2:T(8,128)S(1)} %get-tuple-element.18), channel_id=1, source_target_pairs={{0,1},{2,3},{4,5},{6,7},{8,9},{10,11},{12,13},{14,15},{16,17},{18,... | collective-permute-start | bytes 15368 | tf_op jit(solution)/shard_map/ppermute | solution.py:19
  19.1 41.3 %collective-permute-start.5 = (f32[1,5,1,256]{3,1,0,2:T(8,128)S(1)}, f32[1,5,1,256]{3,1,0,2:T(8,128)S(1)}, u32[]{:S(2)}, u32[]{:S(2)}) collective-permute-start(f32[1,5,1,256]{3,1,0,2:T(8,128)S(1)} %get-tuple-element.17), channel_id=1, source_target_pairs={{1,0},{3,2},{5,4},{7,6},{9,8},{11,10},{13,12},{15,14},{17,16},{19,... | collective-permute-start | bytes 15368 | tf_op jit(solution)/shard_map/ppermute | solution.py:20
  20.4 40.1 %collective-permute-start.4 = (f32[1,5,1,256]{3,1,0,2:T(8,128)S(1)}, f32[1,5,1,256]{3,1,0,2:T(8,128)S(1)}, u32[]{:S(2)}, u32[]{:S(2)}) collective-permute-start(f32[1,5,1,256]{3,1,0,2:T(8,128)S(1)} %get-tuple-element.16), channel_id=1, source_target_pairs={{0,1},{2,3},{4,5},{6,7},{8,9},{10,11},{12,13},{14,15},{16,17},{18,... | collective-permute-start | bytes 15368 | tf_op jit(solution)/shard_map/ppermute | solution.py:19
  60.7 4.4 %collective-permute-start.7 = (f32[1,5,1,256]{3,1,0,2:T(8,128)S(1)}, f32[1,5,1,256]{3,1,0,2:T(8,128)S(1)}, u32[]{:S(2)}, u32[]{:S(2)}) collective-permute-start(f32[1,5,1,256]{3,1,0,2:T(8,128)S(1)} %get-tuple-element.15), channel_id=1, source_target_pairs={{1,0},{3,2},{5,4},{7,6},{9,8},{11,10},{13,12},{15,14},{17,16},{19,... | collective-permute-start | bytes 15368 | tf_op jit(solution)/shard_map/ppermute | solution.py:20
  62.0 3.8 %collective-permute-start.6 = (f32[1,5,1,256]{3,1,0,2:T(8,128)S(1)}, f32[1,5,1,256]{3,1,0,2:T(8,128)S(1)}, u32[]{:S(2)}, u32[]{:S(2)}) collective-permute-start(f32[1,5,1,256]{3,1,0,2:T(8,128)S(1)} %get-tuple-element.14), channel_id=1, source_target_pairs={{0,1},{2,3},{4,5},{6,7},{8,9},{10,11},{12,13},{14,15},{16,17},{18,... | collective-permute-start | bytes 15368 | tf_op jit(solution)/shard_map/ppermute | solution.py:19
  66.8 16.3 %all-to-all-start = ((f32[1,5,16,256]{3,1,0,2:T(8,128)}), f32[1,5,16,256]{3,1,0,2:T(8,128)S(1)}, u32[]{:S(2)}, u32[]{:S(2)}) async-start(f32[1,5,16,256]{3,1,0,2:T(8,128)} %fusion.39), calls=%async_computation | async-start | bytes 262144 | tf_op jit(solution)/shard_map/all_to_all | solution.py:140
  75.1 66.0 %all-gather.5.cloned.1.call-start = ((), (), s32[]{:S(2)}) async-start(), calls=%async_computation.1 | async-start | bytes 2162688 | tf_op jit(solution)/shard_map/all_gather | solution.py:155
  87.0 6.4 %copy-start.1 = (f32[2048]{0:T(1024)S(1)}, f32[2048]{0:T(1024)}, u32[]{:S(2)}) copy-start(f32[2048]{0:T(1024)} %param.16) | copy-start | bytes 24580
  87.0 126.7 %all-gather.7.cloned.1.call-start = ((), (), s32[]{:S(2)}) async-start(), calls=%async_computation.2 | async-start | bytes 2162688 | tf_op jit(solution)/shard_map/all_gather | solution.py:155
  93.4 6.3 %copy-start.9 = (s32[5,5]{1,0:T(8,128)S(1)}, s32[5,5]{1,0:T(8,128)}, u32[]{:S(2)}) copy-start(s32[5,5]{1,0:T(8,128)} %param.17) | copy-start | bytes 304
  141.1 2.2 copy-start.2
  143.5 3.4 %copy-start.8 = (f32[256,256]{1,0:T(8,128)S(1)}, f32[256,256]{1,0:T(8,128)}, u32[]{:S(2)}) copy-start(f32[256,256]{1,0:T(8,128)} %get-tuple-element.62) | copy-start | bytes 786436
  147.0 2.5 %copy-start.7 = (f32[256,256]{1,0:T(8,128)S(1)}, f32[256,256]{1,0:T(8,128)}, u32[]{:S(2)}) copy-start(f32[256,256]{1,0:T(8,128)} %get-tuple-element.63) | copy-start | bytes 786436
  149.4 2.4 %copy-start.6 = (f32[256,256]{1,0:T(8,128)S(1)}, f32[256,256]{1,0:T(8,128)}, u32[]{:S(2)}) copy-start(f32[256,256]{1,0:T(8,128)} %get-tuple-element.64) | copy-start | bytes 786436
  213.7 2.5 %copy-start.3 = (f32[512,1024]{1,0:T(8,128)S(1)}, f32[512,1024]{1,0:T(8,128)}, u32[]{:S(2)}) copy-start(f32[512,1024]{1,0:T(8,128)} %all-gather.7.cloned.1.call-done) | copy-start | bytes 6291460
  219.7 1.3 copy-start.5
  221.1 1.3 copy-start.4
Sparse Core Ops, SparseCore 0:
  87.1 53.9 all-gather.4
  158.3 55.2 all-gather.6
